TPU v7x, 128 devices: a whole 4x4x4 slice. The times are simulated.
128 devices in a mesh: dp: 16 (over y, z), mp: 8 (over x, core).
Axes of the slice: x: 4, y: 4, z: 4, core: 2. Of those that a mesh axis runs over, the one named last changes fastest.
Arguments:
- hidden_in: bfloat16 [4096, 2304], P('dp'), may hold values from -6 to 6
- attn_gain: float32 [2304], replicated, may hold values from 0.25 to 1.75
- w_query: bfloat16 [2304, 2048], P(None, 'mp'), may hold values from -0.25 to 0.25
- w_key: bfloat16 [2304, 2048], P(None, 'mp'), may hold values from -0.125 to 0.125
- w_value: bfloat16 [2304, 2048], P(None, 'mp'), may hold values from -0.125 to 0.125
- w_out: bfloat16 [2048, 2304], P('mp'), may hold values from -0.5 to 0.5
- root_cache: bfloat16 [2, 4096, 2048], P(None, 'dp', 'mp'), may hold values from -400 to 400
- mid_cache: bfloat16 [2, 16, 1024, 2048], P(None, 'dp', None, 'mp'), may hold values from -400 to 400
- leaf_cache: bfloat16 [2, 32, 1024, 2048], P(None, 'dp', None, 'mp'), may hold values from -400 to 400
- mid_len: int32 [16], P('dp'), may hold values from 1 to 1024, 8192 in all
- leaf_len: int32 [32], P('dp'), may hold values from 1 to 1024, 16384 in all
- leaf_of: int32 [128], P('dp'), may hold values from 0 to 31, as said below
- parents: int32 [32], replicated, may hold values from 0 to 15, as said below
- suffix_len: int32 [128], P('dp'), may hold values from 1 to 32, 3072 in all
- ffn_gain: float32 [2304], replicated, may hold values from 0.25 to 1.75
- w_router: float32 [2304, 8], replicated, may hold values from -0.5 to 0.5
- routes: int32 [4096, 2], P('dp'), may hold values from 0 to 7, all different within a row; in each aligned block of 256 rows (0 to 255, 256 to 511, ...) at most 96 rows name the same one
- w_gate: bfloat16 [8, 2304, 5760], P('mp', None, 'dp'), may hold values from -0.125 to 0.125
- w_up: bfloat16 [8, 2304, 5760], P('mp', None, 'dp'), may hold values from -0.125 to 0.125
- w_down: bfloat16 [8, 5760, 2304], P('mp', 'dp'), may hold values from -0.078125 to 0.078125
Outputs:
- layer_out: bfloat16 [4096, 2304], P(('dp', 'mp'))
Inputs may be any that keep to these rules, and one draw needn't show every extreme that they name: `leaf_of`: leaf n belongs to index n // 2 of dp, mid-level node n to index n. The 8 sequences of one index of dp have different mid-level nodes and leaves of one parity, so that no two of them share a mid-level node or a leaf's owner. `parents`: every mid-level node is the parent of exactly one even and one odd leaf. `routes`: in the rows of one index of dp no expert is named by more than 96 rows; some indices of dp reach 96.
All inputs are finite; a program needn't handle non-finite values. No bound on the sum of `mid_len` or of `leaf_len` or of `suffix_len` on one device may be relied on, other than what follows from the above.
Results may differ from a plain program's by a relative error of at most 0.015.
The roundings to bfloat16 on the way count: a program that leaves them out, or rounds other values in their place, can miss the bound.
Values may be sent and summed in bfloat16 or wider, within the bound.
A program may use at most 128 MiB of HBM per device.

v0:
```python
import math
import jax
import jax.numpy as jnp
from jax import lax
from jax.sharding import PartitionSpec as P

HD = 64
TOP = 2
EPS = 1e-05
NEGATIVE = -1e30


def rms_scale(rows, gain):
    rows_wide = rows.astype(jnp.float32)
    mean_square = jnp.mean(rows_wide * rows_wide, axis=-1, keepdims=True)
    return rows_wide * lax.rsqrt(mean_square + EPS) * gain


def level_partial(queries, node_keys, node_values, limits, heads_here, batched):
    senders, row_count, width = queries.shape
    head_dim = width // heads_here
    scale = 1.0 / math.sqrt(head_dim)
    query_heads = queries.reshape(senders, row_count, heads_here, head_dim)
    if batched:
        key_heads = node_keys.reshape(senders, -1, heads_here, head_dim)
        value_heads = node_values.reshape(senders, -1, heads_here, head_dim)
        scores = jnp.einsum(
            "sqhd,skhd->sqhk", query_heads, key_heads, preferred_element_type=jnp.float32
        )
    else:
        key_heads = node_keys.reshape(-1, heads_here, head_dim)
        value_heads = node_values.reshape(-1, heads_here, head_dim)
        scores = jnp.einsum(
            "sqhd,khd->sqhk", query_heads, key_heads, preferred_element_type=jnp.float32
        )
    scores = scores * scale
    slots = jnp.arange(scores.shape[-1], dtype=jnp.int32)
    allowed = slots[None, :] < limits[:, None]
    scores = jnp.where(allowed[:, None, None, :], scores, NEGATIVE)
    peak = jnp.max(scores, axis=-1)
    weights = jnp.exp(scores - peak[..., None])
    total = jnp.sum(weights, axis=-1)
    probs = weights.astype(jnp.bfloat16)
    if batched:
        summed = jnp.einsum(
            "sqhk,skhd->sqhd", probs, value_heads, preferred_element_type=jnp.float32
        )
    else:
        summed = jnp.einsum(
            "sqhk,khd->sqhd", probs, value_heads, preferred_element_type=jnp.float32
        )
    result = (summed / total[..., None]).reshape(senders, row_count, width)
    return (result, peak + jnp.log(total))


def on_device(
    hidden_in,
    attn_gain,
    w_query,
    w_key,
    w_value,
    w_out,
    root_cache,
    mid_cache,
    leaf_cache,
    mid_len,
    leaf_len,
    leaf_of,
    parents,
    suffix_len,
    ffn_gain,
    w_router,
    routes,
    w_gate,
    w_up,
    w_down,
):
    tok_rows, width = hidden_in.shape
    seq_rows = suffix_len.shape[0]
    suffix = tok_rows // seq_rows
    head_dim = HD
    local_width = w_query.shape[1]
    heads_here = local_width // head_dim
    scale = 1.0 / math.sqrt(head_dim)
    owners = lax.axis_size("dp")
    normed = rms_scale(hidden_in, attn_gain).astype(jnp.bfloat16)
    query = jnp.dot(normed, w_query, preferred_element_type=jnp.float32).astype(jnp.bfloat16)
    key = jnp.dot(normed, w_key, preferred_element_type=jnp.float32).astype(jnp.bfloat16)
    value = jnp.dot(normed, w_value, preferred_element_type=jnp.float32).astype(jnp.bfloat16)
    query_heads = query.reshape(tok_rows, heads_here, head_dim)
    piece = lax.all_gather(root_cache, "dp", axis=1, tiled=True)
    running_peak = jnp.full((tok_rows, heads_here), NEGATIVE, jnp.float32)
    piece_keys = piece[0].reshape(-1, heads_here, head_dim)
    piece_values = piece[1].reshape(-1, heads_here, head_dim)
    scores = (
        jnp.einsum("qhd,khd->qhk", query_heads, piece_keys, preferred_element_type=jnp.float32)
        * scale
    )
    new_peak = jnp.maximum(running_peak, jnp.max(scores, axis=-1))
    weights = jnp.exp(scores - new_peak[..., None])
    new_total = jnp.sum(weights, axis=-1)
    added = jnp.einsum(
        "qhk,khd->qhd",
        weights.astype(jnp.bfloat16),
        piece_values,
        preferred_element_type=jnp.float32,
    )
    root_out = added / new_total[..., None]
    root_lse = new_peak + jnp.log(new_total)
    query_seq = query.reshape(seq_rows, suffix, heads_here, head_dim)
    key_seq = key.reshape(seq_rows, suffix, heads_here, head_dim)
    value_seq = value.reshape(seq_rows, suffix, heads_here, head_dim)
    slots = jnp.arange(suffix, dtype=jnp.int32)
    self_ok = (slots[None, None, :] <= slots[None, :, None]) & (
        slots[None, None, :] < suffix_len[:, None, None]
    )
    self_scores = (
        jnp.einsum("sqhd,skhd->sqhk", query_seq, key_seq, preferred_element_type=jnp.float32)
        * scale
    )
    self_scores = jnp.where(self_ok[:, :, None, :], self_scores, NEGATIVE)
    self_peak = jnp.max(self_scores, axis=-1)
    self_weights = jnp.exp(self_scores - self_peak[..., None])
    self_total = jnp.sum(self_weights, axis=-1)
    self_sum = jnp.einsum(
        "sqhk,skhd->sqhd",
        self_weights.astype(jnp.bfloat16),
        value_seq,
        preferred_element_type=jnp.float32,
    )
    self_out = (self_sum / self_total[..., None]).reshape(tok_rows, heads_here, head_dim)
    self_lse = (self_peak + jnp.log(self_total)).reshape(tok_rows, heads_here)
    mid_of = parents[leaf_of]
    leaf_owner = leaf_of // 2
    targets = jnp.arange(owners, dtype=jnp.int32)
    pick_mid = (mid_of[None, :] == targets[:, None]).astype(jnp.bfloat16)
    pick_leaf = (leaf_owner[None, :] == targets[:, None]).astype(jnp.bfloat16)
    flat_query = query.reshape(seq_rows, suffix * local_width)
    sent_mid = jnp.dot(pick_mid, flat_query, preferred_element_type=jnp.float32).astype(
        jnp.bfloat16
    )
    sent_leaf = jnp.dot(pick_leaf, flat_query, preferred_element_type=jnp.float32).astype(
        jnp.bfloat16
    )
    sent = jnp.stack([sent_mid, sent_leaf], axis=1).reshape(owners, 2, suffix, local_width)
    sent_queries = lax.all_to_all(sent, "dp", split_axis=0, concat_axis=0, tiled=True)
    leaf_every = lax.all_gather(leaf_of, "dp", axis=0, tiled=True).reshape(owners, seq_rows)
    me_dp = lax.axis_index("dp")
    second = jnp.any((leaf_every // 2 == me_dp) & (leaf_every % 2 == 1), axis=1)
    senders = sent_queries.shape[0]
    mid_limit = jnp.broadcast_to(mid_len[0], (senders,))
    mid_result, mid_logsum = level_partial(
        sent_queries[:, 0], mid_cache[0, 0], mid_cache[1, 0], mid_limit, heads_here, False
    )
    leaf_keys = jnp.where(second[:, None, None], leaf_cache[0, 1][None], leaf_cache[0, 0][None])
    leaf_values = jnp.where(second[:, None, None], leaf_cache[1, 1][None], leaf_cache[1, 0][None])
    leaf_limit = jnp.where(second, leaf_len[1], leaf_len[0])
    leaf_result, leaf_logsum = level_partial(
        sent_queries[:, 1], leaf_keys, leaf_values, leaf_limit, heads_here, True
    )
    owner_out = jnp.stack([mid_result, leaf_result], axis=1)
    owner_lse = jnp.stack([mid_logsum, leaf_logsum], axis=1)
    owner_all = jnp.concatenate([owner_out, owner_lse], axis=-1)
    back_all = lax.all_to_all(owner_all, "dp", split_axis=0, concat_axis=0, tiled=True)
    back_out = back_all[..., :local_width]
    back_lse = back_all[..., local_width:]
    mid_out = back_out[mid_of, 0].reshape(tok_rows, heads_here, head_dim)
    mid_lse = back_lse[mid_of, 0].reshape(tok_rows, heads_here)
    leaf_out = back_out[leaf_owner, 1].reshape(tok_rows, heads_here, head_dim)
    leaf_lse = back_lse[leaf_owner, 1].reshape(tok_rows, heads_here)
    stacked_lse = jnp.stack([root_lse, mid_lse, leaf_lse, self_lse])
    stacked_out = jnp.stack([root_out, mid_out, leaf_out, self_out])
    overall = jnp.max(stacked_lse, axis=0)
    shares = jnp.exp(stacked_lse - overall)
    combined = jnp.sum(shares[..., None] * stacked_out, axis=0) / jnp.sum(shares, axis=0)[..., None]
    attended = combined.reshape(tok_rows, local_width).astype(jnp.bfloat16)
    projected = jnp.dot(attended, w_out, preferred_element_type=jnp.float32)
    rows_here = tok_rows // lax.axis_size("mp")
    first = lax.axis_index("mp") * rows_here
    attn_rows = lax.psum_scatter(projected, "mp", scatter_dimension=0, tiled=True)
    resid = lax.dynamic_slice_in_dim(hidden_in, first, rows_here, 0).astype(jnp.float32) + attn_rows
    ffn_rows = rms_scale(resid, ffn_gain).astype(jnp.bfloat16)
    ffn_in = lax.all_gather(ffn_rows, "mp", axis=0, tiled=True)
    logits = jnp.dot(ffn_in.astype(jnp.float32), w_router, precision=lax.Precision.HIGHEST)
    chosen = jnp.take_along_axis(logits, routes, axis=1)
    squashed = jax.nn.sigmoid(chosen)
    gates = squashed / jnp.sum(squashed, axis=1, keepdims=True)
    expert = lax.axis_index("mp")
    hit_each = routes == expert
    hit = jnp.any(hit_each, axis=1)
    gate_here = jnp.sum(jnp.where(hit_each, gates, 0.0), axis=1)
    order = jnp.cumsum(hit.astype(jnp.int32)) - 1
    capacity = 3 * TOP * tok_rows // (2 * lax.axis_size("mp"))
    slot_ids = jnp.arange(capacity, dtype=jnp.int32)
    pick_slot = (order[None, :] == slot_ids[:, None]) & hit[None, :]
    dispatch = jnp.dot(
        pick_slot.astype(jnp.bfloat16), ffn_in, preferred_element_type=jnp.float32
    ).astype(jnp.bfloat16)
    slot_gate = jnp.dot(pick_slot.astype(jnp.float32), gate_here, precision=lax.Precision.HIGHEST)
    gate_weight = w_gate[0]
    up_weight = w_up[0]
    down_weight = w_down[0]
    piece = lax.all_gather(dispatch, "dp", axis=0, tiled=True)
    gate_part = jnp.dot(piece, gate_weight, preferred_element_type=jnp.float32)
    up_part = jnp.dot(piece, up_weight, preferred_element_type=jnp.float32)
    partial_out = jnp.dot(
        (jax.nn.silu(gate_part) * up_part).astype(jnp.bfloat16),
        down_weight,
        preferred_element_type=jnp.float32,
    )
    expert_out = lax.psum_scatter(
        partial_out.astype(jnp.bfloat16), "dp", scatter_dimension=0, tiled=True
    )
    weighted = expert_out.astype(jnp.float32) * slot_gate[:, None]
    spread = jnp.dot(pick_slot.astype(jnp.float32).T, weighted, precision=lax.Precision.HIGHEST)
    mixed = lax.psum_scatter(
        spread.astype(jnp.bfloat16), "mp", scatter_dimension=0, tiled=True
    ).astype(jnp.float32)
    row_ids = first + jnp.arange(rows_here, dtype=jnp.int32)
    valid = row_ids % suffix < suffix_len[row_ids // suffix]
    return jnp.where(valid[:, None], resid + mixed, 0.0).astype(jnp.bfloat16)


def solution(mesh):
    return jax.shard_map(
        on_device,
        mesh=mesh,
        in_specs=(
            P("dp", None),
            P(),
            P(None, "mp"),
            P(None, "mp"),
            P(None, "mp"),
            P("mp", None),
            P(None, "dp", "mp"),
            P(None, "dp", None, "mp"),
            P(None, "dp", None, "mp"),
            P("dp"),
            P("dp"),
            P("dp"),
            P(),
            P("dp"),
            P(),
            P(),
            P("dp", None),
            P("mp", None, "dp"),
            P("mp", None, "dp"),
            P("mp", "dp", None),
        ),
        out_specs=P(("dp", "mp"), None),
        check_vma=False,
    )
```

profile of v0, /device:TPU:0, one launch (start us, length us, event | category | flops | bytes accessed | tf_op | source)
XLA Modules:
  0.0 436.8 jit_solution(13475134126374077228)
XLA Ops:
  14.9 8.2 %all-to-all-start = ((bf16[16,2,32,256]{3,2,1,0:T(8,128)(2,1)}), bf16[16,2,32,256]{3,2,1,0:T(8,128)(2,1)}, u32[]{:S(2)}, u32[]{:S(2)}) async-start(bf16[16,2,32,256]{3,2,1,0:T(8,128)(2,1)} %pad_maximum_fusion.1), calls=%async_computation | async-start | bytes 1048576 | tf_op jit(solution)/shard_map/all_to_all | solution.py:146
  24.6 17.4 %all-reduce.2 = s32[128]{0:T(128)S(1)} all-reduce(s32[128]{0:T(128)S(1)} %dynamic-update-slice), channel_id=1, replica_groups=mesh['dp'=16,'mp'=8] {'dp'}, use_global_device_ids=true, to_apply=%add.2 | all-reduce | flops 128 | bytes 1024
  47.2 2.5 convolution_convert_fusion.6
  64.6 4.3 bitcast_reduce_fusion.1
  68.9 2.6 fusion.15
  71.6 2.7 fusion.58
  87.6 5.1 %all-to-all-start.1 = ((f32[16,2,32,260]{3,2,1,0:T(8,128)}), f32[16,2,32,260]{3,2,1,0:T(8,128)S(1)}, u32[]{:S(2)}, u32[]{:S(2)}) async-start(f32[16,2,32,260]{3,2,1,0:T(8,128)} %pad_maximum_fusion), calls=%async_computation.1 | async-start | bytes 3145728 | tf_op jit(solution)/shard_map/all_to_all | solution.py:164
  94.3 2.8 convolution_convert_fusion.5
  102.3 10.9 %all-to-all-done.1 = f32[16,2,32,260]{3,2,1,0:T(8,128)S(1)} async-done(((f32[16,2,32,260]{3,2,1,0:T(8,128)}), f32[16,2,32,260]{3,2,1,0:T(8,128)S(1)}, u32[]{:S(2)}, u32[]{:S(2)}) %all-to-all-start.1) | async-done | bytes 1064992 | tf_op jit(solution)/shard_map/all_to_all | solution.py:164
  122.5 4.5 %fusion.124 = (bf16[1,4096,256]{2,1,0:T(8,128)(2,1)}, bf16[1,4096,256]{2,1,0:T(8,128)(2,1)}) fusion(bf16[2,4096,256]{2,1,0:T(8,128)(2,1)} %all-gather.4.cloned.1.call-done), kind=kLoop, calls=%fused_computation.185 | loop fusion | bytes 8388608 | tf_op jit(solution)/shard_map/slice | solution.py:93
  127.0 4.1 copy.253
  131.1 4.2 copy.282
  135.2 9.7 %bitcast_reduce_fusion = (f32[256,4]{0,1:T(4,128)S(1)}, f32[4,256,4096]{2,1,0:T(8,128)}) fusion(bf16[256,4,64]{0,2,1:T(8,128)(2,1)S(1)} %bitcast.190, bf16[4096,4,64]{0,2,1:T(8,128)(2,1)} %bitcast.174), kind=kOutput, calls=%fused_computation.8 | convolution fusion | flops 545258496 | bytes 19009536 | tf_op jit(solution)/shard_map/qhd,khd->qhk/dot_general | solution.py:96
  144.9 8.6 %fusion.2 = f32[256,4]{0,1:T(4,128)S(1)} fusion(f32[4,256,4096]{2,1,0:T(8,128)} %get-tuple-element.33, f32[256,4]{0,1:T(4,128)S(1)} %broadcast_maximum_fusion), kind=kLoop, calls=%fused_computation.11 | loop fusion | flops 12581888 | bytes 16785408 | tf_op jit(solution)/shard_map/reduce_sum | solution.py:101
  153.6 8.1 %fusion.54 = f32[1,256,4,64]{1,3,2,0:T(8,128)S(1)} fusion(bf16[4096,4,64]{0,2,1:T(8,128)(2,1)} %bitcast.176, f32[4,256,4096]{2,1,0:T(8,128)} %get-tuple-element.33, f32[256,4]{0,1:T(4,128)S(1)} %broadcast_maximum_fusion, f32[256,4]{0,1:T(4,128)S(1)} %fusion.2), kind=kOutput, calls=%fused_computation.71 | convolution fusion | flops 549519360 | bytes 19144704 | tf_op jit(solution)/shard_map/qhk,khd->qhd/dot_general | solution.py:102
  165.0 31.7 %reduce-scatter.4.cloned.1.call-done = f32[32,2304]{1,0:T(8,128)} async-done(((f32[256,2304]{1,0:T(8,128)}), f32[32,2304]{1,0:T(8,128)}) %reduce-scatter.4.cloned.1.call-update) | async-done | bytes 294928 | tf_op jit(solution)/shard_map/reduce_scatter | solution.py:180
  200.3 21.9 %all-gather.6.cloned.1.call-done = bf16[256,2304]{1,0:T(8,128)(2,1)} async-done(((bf16[32,2304]{1,0:T(8,128)(2,1)}), bf16[256,2304]{1,0:T(8,128)(2,1)}) %all-gather.6.cloned.1.call-update) | async-done | bytes 1179664 | tf_op jit(solution)/shard_map/all_gather | solution.py:183
  224.9 65.0 %all-gather.8.cloned.1.call-done = bf16[1536,2304]{1,0:T(8,128)(2,1)} async-done(((bf16[96,2304]{1,0:T(8,128)(2,1)}), bf16[1536,2304]{1,0:T(8,128)(2,1)}) %all-gather.8.cloned.1.call-update) | async-done | bytes 7077904 | tf_op jit(solution)/shard_map/all_gather | solution.py:203
  289.9 7.6 %fusion.35 = f32[1536,360]{0,1:T(8,128)} fusion(bf16[1536,2304]{1,0:T(8,128)(2,1)} %all-gather.8.cloned.1.call-done, bf16[1,2304,360]{1,2,0:T(8,128)(2,1)} %param.37), kind=kOutput, calls=%fused_computation.55 | convolution fusion | flops 2548039680 | bytes 10948608 | tf_op jit(solution)/shard_map/dot_general | solution.py:204
  297.5 13.1 %convolution_convert_fusion = bf16[1536,2304]{1,0:T(8,128)(2,1)} fusion(bf16[1,360,2304]{2,1,0:T(8,128)(2,1)S(1)} %copy-done, bf16[1536,2304]{1,0:T(8,128)(2,1)} %all-gather.8.cloned.1.call-done, f32[1536,360]{0,1:T(8,128)} %fusion.35, bf16[1,2304,360]{1,2,0:T(8,128)(2,1)} %param.38), kind=kOutput, calls=%fused_computation.12 | convolution fusion | flops 5102936064 | bytes 19685376 | tf_op jit(solution)/shard_map/dot_general | solution.py:206
  312.9 3.6 gather_fusion.6
  316.9 76.4 %reduce-scatter.6.cloned.1.call-done = bf16[96,2304]{1,0:T(8,128)(2,1)} async-done(((bf16[1536,2304]{1,0:T(8,128)(2,1)}), bf16[96,2304]{1,0:T(8,128)(2,1)}) %reduce-scatter.6.cloned.1.call-update) | async-done | bytes 442384 | tf_op jit(solution)/shard_map/reduce_scatter | solution.py:211
  393.3 3.2 convolution_convert_fusion.3
  397.3 30.7 %reduce-scatter.8.cloned.1.call-done = bf16[32,2304]{1,0:T(8,128)(2,1)} async-done(((bf16[256,2304]{1,0:T(8,128)(2,1)}), bf16[32,2304]{1,0:T(8,128)(2,1)}) %reduce-scatter.8.cloned.1.call-update) | async-done | bytes 147472 | tf_op jit(solution)/shard_map/reduce_scatter | solution.py:216
  (175 shorter events, 72.3 us)
Async XLA Ops:
  6.5 290.9 %copy-start = (bf16[1,360,2304]{2,1,0:T(8,128)(2,1)S(1)}, bf16[1,360,2304]{2,1,0:T(8,128)(2,1)}, u32[]{:S(2)}) copy-start(bf16[1,360,2304]{2,1,0:T(8,128)(2,1)} %param.39) | copy-start | bytes 4976644
  6.5 116.0 %all-gather.4.cloned.1.call-start = ((), (), s32[]{:S(2)}) async-start(), calls=%async_computation.5 | async-start | bytes 4456448 | tf_op jit(solution)/shard_map/all_gather | solution.py:91
  12.7 10.4 %copy-start.26 = (u32[128]{0:T(128)S(1)}, u32[128]{0:T(128)}, u32[]{:S(2)}) copy-start(u32[128]{0:T(128)} %constant.214) | copy-start | bytes 1540
  12.7 11.7 %copy-start.24 = (s32[8]{0:T(128)S(1)}, s32[8]{0:T(128)}, u32[]{:S(2)}) copy-start(s32[8]{0:T(128)} %param.31) | copy-start | bytes 100
  12.7 29.3 %copy-start.3 = (s32[8]{0:T(128)S(1)}, s32[8]{0:T(128)}, u32[]{:S(2)}) copy-start(s32[8]{0:T(128)} %param.33) | copy-start | bytes 100
  12.7 29.3 %copy-start.23 = (s32[2]{0:T(128)S(1)}, s32[2]{0:T(128)}, u32[]{:S(2)}) copy-start(s32[2]{0:T(128)} %param.30) | copy-start | bytes 28
  14.0 33.2 %copy-start.6 = (bf16[256,2304]{1,0:T(8,128)(2,1)S(1)}, bf16[256,2304]{1,0:T(8,128)(2,1)}, u32[]{:S(2)}) copy-start(bf16[256,2304]{1,0:T(8,128)(2,1)} %param.20) | copy-start | bytes 3538948
  14.9 47.3 %all-to-all-start = ((bf16[16,2,32,256]{3,2,1,0:T(8,128)(2,1)}), bf16[16,2,32,256]{3,2,1,0:T(8,128)(2,1)}, u32[]{:S(2)}, u32[]{:S(2)}) async-start(bf16[16,2,32,256]{3,2,1,0:T(8,128)(2,1)} %pad_maximum_fusion.1), calls=%async_computation | async-start | bytes 1048576 | tf_op jit(solution)/shard_map/all_to_all | solution.py:146
  44.9 4.7 %copy-start.7 = (bf16[2,2,1024,256]{3,2,1,0:T(8,128)(2,1)S(1)}, bf16[2,2,1024,256]{3,2,1,0:T(8,128)(2,1)}, u32[]{:S(2)}) copy-start(bf16[2,2,1024,256]{3,2,1,0:T(8,128)(2,1)} %param.28) | copy-start | bytes 6291460
  53.8 4.2 copy-start.10
  53.8 6.4 %copy-start.18 = (bf16[8,32,4,64]{3,2,1,0:T(4,128)(2,1)S(1)}, bf16[8,32,4,64]{3,2,1,0:T(4,128)(2,1)}, u32[]{:S(2)}) copy-start(bf16[8,32,4,64]{3,2,1,0:T(4,128)(2,1)} %reshape.404) | copy-start | bytes 393220
  87.6 6.6 %copy-start.25 = (f32[2304]{0:T(1024)S(1)}, f32[2304]{0:T(1024)}, u32[]{:S(2)}) copy-start(f32[2304]{0:T(1024)} %param.21) | copy-start | bytes 27652
  87.6 25.6 %all-to-all-start.1 = ((f32[16,2,32,260]{3,2,1,0:T(8,128)}), f32[16,2,32,260]{3,2,1,0:T(8,128)S(1)}, u32[]{:S(2)}, u32[]{:S(2)}) async-start(f32[16,2,32,260]{3,2,1,0:T(8,128)} %pad_maximum_fusion), calls=%async_computation.1 | async-start | bytes 3145728 | tf_op jit(solution)/shard_map/all_to_all | solution.py:164
  92.7 104.0 %reduce-scatter.4.cloned.1.call-start = ((), (), s32[]{:S(2)}) async-start(), calls=%async_computation.6 | async-start | bytes 2654208 | tf_op jit(solution)/shard_map/reduce_scatter | solution.py:180
  131.1 4.2 copy-start.17
  153.6 8.2 %copy-start.12 = (f32[1,256,4,64]{1,3,2,0:T(8,128)S(1)}, f32[1,256,4,64]{1,3,2,0:T(8,128)}, u32[]{:S(2)}) copy-start(f32[1,256,4,64]{1,3,2,0:T(8,128)} %copy.288) | copy-start | bytes 786436
  163.0 34.8 %copy-start.22 = (f32[2304]{0:T(1024)S(1)}, f32[2304]{0:T(1024)}, u32[]{:S(2)}) copy-start(f32[2304]{0:T(1024)} %param.34) | copy-start | bytes 27652
  164.9 34.8 %copy-start.21 = (s32[256,2]{0,1:T(2,128)S(1)}, s32[256,2]{0,1:T(2,128)}, u32[]{:S(2)}) copy-start(s32[256,2]{0,1:T(2,128)} %param.36) | copy-start | bytes 6148
  164.9 57.3 %all-gather.6.cloned.1.call-start = ((), (), s32[]{:S(2)}) async-start(), calls=%async_computation.7 | async-start | bytes 1327104 | tf_op jit(solution)/shard_map/all_gather | solution.py:183
  199.6 90.3 %all-gather.8.cloned.1.call-start = ((), (), s32[]{:S(2)}) async-start(), calls=%async_computation.8 | async-start | bytes 7520256 | tf_op jit(solution)/shard_map/all_gather | solution.py:203
  224.6 168.7 %reduce-scatter.6.cloned.1.call-start = ((), (), s32[]{:S(2)}) async-start(), calls=%async_computation.9 | async-start | bytes 7520256 | tf_op jit(solution)/shard_map/reduce_scatter | solution.py:211
  310.6 117.3 %reduce-scatter.8.cloned.1.call-start = ((), (), s32[]{:S(2)}) async-start(), calls=%async_computation.10 | async-start | bytes 1327104 | tf_op jit(solution)/shard_map/reduce_scatter | solution.py:216
  312.9 116.8 %copy-start.1 = (bf16[1,360,2304]{2,1,0:T(8,128)(2,1)S(1)}, bf16[1,360,2304]{2,1,0:T(8,128)(2,1)}, u32[]{:S(2)}) copy-start(bf16[1,360,2304]{2,1,0:T(8,128)(2,1)} %param.39) | copy-start | bytes 4976644
  316.4 111.5 %copy-start.5 = (f32[32,2304]{1,0:T(8,128)S(1)}, f32[32,2304]{1,0:T(8,128)}, u32[]{:S(2)}) copy-start(f32[32,2304]{1,0:T(8,128)} %reduce-scatter.4.cloned.1.call-done) | copy-start | bytes 884740
  (11 other events, 23.9 us)
Sparse Core Ops, SparseCore 0:
  9.6 57.6 all-gather.3
  165.0 31.5 reduce-scatter.3
  199.7 22.4 all-gather.5
  224.7 65.1 all-gather.7
  310.8 82.4 reduce-scatter.5
  396.6 31.2 reduce-scatter.7
where the time goes:
time: 444 us; the launch traced here: 437 us
  waiting for transfers between devices  237 us (53%)
  matrix products  69.9 us (16%)
  local copies, waits for them, and re-layouts  55.5 us (12%)
  other arithmetic  27.1 us (6%)
  blocking collectives  17.4 us (4%)
  between operations  15.6 us (4%)
  starting transfers between devices  13.8 us (3%)
    reduce_scatter x1, waiting for transfers between devices, on_device(): lax.psum_scatter(partial_out.astype(jnp.bfloat16), 'dp', scatter_dimensio...  76.4 us
    all_gather x1, waiting for transfers between devices, on_device(): piece = lax.all_gather(dispatch, 'dp', axis=0, tiled=True)  65 us
    reduce_scatter x1, waiting for transfers between devices, on_device(): lax.psum_scatter(projected, 'mp', scatter_dimension=0, tiled=True)  31.7 us
    reduce_scatter x1, waiting for transfers between devices, on_device(): lax.psum_scatter(spread.astype(jnp.bfloat16), 'mp', scatter_dimension=0,...  30.7 us
    all_gather x1, waiting for transfers between devices, on_device(): ffn_in = lax.all_gather(ffn_rows, 'mp', axis=0, tiled=True)  21.9 us
    unnamed x1, blocking collectives  17.4 us
    dot_general x1, matrix products, on_device(): jnp.dot((jax.nn.silu(gate_part) * up_part).astype(jnp.bfloat16), down_wei...  13.1 us
    unnamed x64, local copies, waits for them, and re-layouts  11.2 us
  transfers between devices with their start and end apart: 8, of which 6 were waited for; matrix products, arithmetic and copies ran while one was open for 18% of the time, Pallas kernels for 0%

commit v1 on v0

--- a/solution.py
+++ b/solution.py
@@ -3,11 +3,19 @@
 import jax.numpy as jnp
 from jax import lax
 from jax.sharding import PartitionSpec as P
+from jax.lax import all_to_all, psum
 
 HD = 64
 TOP = 2
 EPS = 1e-05
 NEGATIVE = -1e30
+
+
+def runs_bring(slab_in, across):
+    val = jnp.stack([slab_in for _ in range(psum(1, across))])
+    reply = all_to_all(val, across, 0, 0)
+    tall = jnp.concatenate(reply, axis=0)
+    return tall
 
 
 def rms_scale(rows, gain):
@@ -200,7 +208,7 @@
     gate_weight = w_gate[0]
     up_weight = w_up[0]
     down_weight = w_down[0]
-    piece = lax.all_gather(dispatch, "dp", axis=0, tiled=True)
+    piece = runs_bring(dispatch, "dp")
     gate_part = jnp.dot(piece, gate_weight, preferred_element_type=jnp.float32)
     up_part = jnp.dot(piece, up_weight, preferred_element_type=jnp.float32)
     partial_out = jnp.dot(

time: 444 us -> 464 us (1.045)
  blocking collectives: 17.4 us -> 106 us
  waiting for transfers between devices: 237 us -> 169 us
    all_to_all x0 -> x1, blocking collectives: none -> 88.9 us  [runs_bring(): reply = all_to_all(val, across, 0, 0)]
    all_gather x1 -> x0, waiting for transfers between devices: 65 us -> none  [on_device(): piece = lax.all_gather(dispatch, 'dp', axis=0, tiled=True)]
    unnamed x64 -> x66, local copies, waits for them, and re-layouts: 11.2 us -> 14.1 us
  transfers between devices with their start and end apart: 8 -> 7, of which waited for: 6 -> 5; matrix products, arithmetic and copies ran while one was open for 18% -> 17% of each run, Pallas kernels for 0% -> 0%
where the time goes in v1:
time: 464 us; the launch traced here: 456 us
  waiting for transfers between devices  169 us (36%)
  blocking collectives  106 us (23%)
  matrix products  65.7 us (14%)
  local copies, waits for them, and re-layouts  59.1 us (13%)
  other arithmetic  27.1 us (6%)
  between operations  15.3 us (3%)
  starting transfers between devices  13.8 us (3%)
    all_to_all x1, blocking collectives, runs_bring(): reply = all_to_all(val, across, 0, 0)  88.9 us
    reduce_scatter x1, waiting for transfers between devices, on_device(): lax.psum_scatter(partial_out.astype(jnp.bfloat16), 'dp', scatter_dimensio...  73.2 us
    reduce_scatter x1, waiting for transfers between devices, on_device(): lax.psum_scatter(projected, 'mp', scatter_dimension=0, tiled=True)  31.7 us
    reduce_scatter x1, waiting for transfers between devices, on_device(): lax.psum_scatter(spread.astype(jnp.bfloat16), 'mp', scatter_dimension=0,...  30.7 us
    all_gather x1, waiting for transfers between devices, on_device(): ffn_in = lax.all_gather(ffn_rows, 'mp', axis=0, tiled=True)  21.8 us
    unnamed x1, blocking collectives  17.4 us
    unnamed x66, local copies, waits for them, and re-layouts  14.1 us
    dot_general x1, matrix products, on_device(): jnp.dot((jax.nn.silu(gate_part) * up_part).astype(jnp.bfloat16), down_wei...  13.1 us
  transfers between devices with their start and end apart: 7, of which 5 were waited for; matrix products, arithmetic and copies ran while one was open for 17% of the time, Pallas kernels for 0%

profile of v1, /device:TPU:0, one launch (start us, length us, event | category | flops | bytes accessed | tf_op | source)
XLA Modules:
  0.0 456.4 jit_solution(16208910190513061712)
XLA Ops:
  14.9 8.2 %all-to-all-start = ((bf16[16,2,32,256]{3,2,1,0:T(8,128)(2,1)}), bf16[16,2,32,256]{3,2,1,0:T(8,128)(2,1)}, u32[]{:S(2)}, u32[]{:S(2)}) async-start(bf16[16,2,32,256]{3,2,1,0:T(8,128)(2,1)} %pad_maximum_fusion.1), calls=%async_computation | async-start | bytes 1048576 | tf_op jit(solution)/shard_map/all_to_all | solution.py:154
  24.6 17.4 %all-reduce.2 = s32[128]{0:T(128)S(1)} all-reduce(s32[128]{0:T(128)S(1)} %dynamic-update-slice), channel_id=1, replica_groups=mesh['dp'=16,'mp'=8] {'dp'}, use_global_device_ids=true, to_apply=%add.2 | all-reduce | flops 128 | bytes 1024
  64.6 4.3 bitcast_reduce_fusion.1
  68.9 2.6 fusion.15
  71.6 2.7 fusion.58
  87.6 5.1 %all-to-all-start.1 = ((f32[16,2,32,260]{3,2,1,0:T(8,128)}), f32[16,2,32,260]{3,2,1,0:T(8,128)S(1)}, u32[]{:S(2)}, u32[]{:S(2)}) async-start(f32[16,2,32,260]{3,2,1,0:T(8,128)} %pad_maximum_fusion), calls=%async_computation.1 | async-start | bytes 3145728 | tf_op jit(solution)/shard_map/all_to_all | solution.py:172
  94.3 2.8 convolution_convert_fusion.5
  102.3 10.9 %all-to-all-done.1 = f32[16,2,32,260]{3,2,1,0:T(8,128)S(1)} async-done(((f32[16,2,32,260]{3,2,1,0:T(8,128)}), f32[16,2,32,260]{3,2,1,0:T(8,128)S(1)}, u32[]{:S(2)}, u32[]{:S(2)}) %all-to-all-start.1) | async-done | bytes 1064992 | tf_op jit(solution)/shard_map/all_to_all | solution.py:172
  122.5 4.5 fusion.124
  127.0 4.1 copy.253
  131.1 4.2 copy.282
  135.2 9.7 %bitcast_reduce_fusion = (f32[256,4]{0,1:T(4,128)S(1)}, f32[4,256,4096]{2,1,0:T(8,128)}) fusion(bf16[256,4,64]{0,2,1:T(8,128)(2,1)S(1)} %bitcast.193, bf16[4096,4,64]{0,2,1:T(8,128)(2,1)} %bitcast.175), kind=kOutput, calls=%fused_computation.8 | convolution fusion | flops 545258496 | bytes 19009536 | tf_op jit(solution)/shard_map/qhd,khd->qhk/dot_general | solution.py:104
  144.9 8.6 %fusion.2 = f32[256,4]{0,1:T(4,128)S(1)} fusion(f32[4,256,4096]{2,1,0:T(8,128)} %get-tuple-element.33, f32[256,4]{0,1:T(4,128)S(1)} %broadcast_maximum_fusion), kind=kLoop, calls=%fused_computation.11 | loop fusion | flops 12581888 | bytes 16785408 | tf_op jit(solution)/shard_map/reduce_sum | solution.py:109
  153.6 8.1 %fusion.54 = f32[1,256,4,64]{1,3,2,0:T(8,128)S(1)} fusion(bf16[4096,4,64]{0,2,1:T(8,128)(2,1)} %bitcast.179, f32[4,256,4096]{2,1,0:T(8,128)} %get-tuple-element.33, f32[256,4]{0,1:T(4,128)S(1)} %broadcast_maximum_fusion, f32[256,4]{0,1:T(4,128)S(1)} %fusion.2), kind=kOutput, calls=%fused_computation.71 | convolution fusion | flops 549519360 | bytes 19144704 | tf_op jit(solution)/shard_map/qhk,khd->qhd/dot_general | solution.py:110
  165.0 31.7 %reduce-scatter.4.cloned.1.call-done = f32[32,2304]{1,0:T(8,128)} async-done(((f32[256,2304]{1,0:T(8,128)}), f32[32,2304]{1,0:T(8,128)}) %reduce-scatter.4.cloned.1.call-update) | async-done | bytes 294928 | tf_op jit(solution)/shard_map/reduce_scatter | solution.py:188
  200.5 21.8 %all-gather.5.cloned.1.call-done = bf16[256,2304]{1,0:T(8,128)(2,1)} async-done(((bf16[32,2304]{1,0:T(8,128)(2,1)}), bf16[256,2304]{1,0:T(8,128)(2,1)}) %all-gather.5.cloned.1.call-update) | async-done | bytes 1179664 | tf_op jit(solution)/shard_map/all_gather | solution.py:191
  224.6 88.9 %all_to_all.15 = bf16[16,96,2304]{2,1,0:T(8,128)(2,1)S(1)} all-to-all(bf16[16,96,2304]{2,1,0:T(8,128)(2,1)S(1)} %stack.60), channel_id=1, replica_groups=mesh['dp'=16,'mp'=8] {'dp'}, dimensions={0} | all-to-all | bytes 14155776 | tf_op jit(solution)/shard_map/all_to_all | solution.py:16
  313.5 2.9 copy-done.3
  316.4 4.1 fusion.35
  320.5 13.1 %convolution_convert_fusion = bf16[1536,2304]{1,0:T(8,128)(2,1)} fusion(bf16[1,360,2304]{2,1,0:T(8,128)(2,1)S(1)} %copy-done, bf16[1536,2304]{1,0:T(8,128)(2,1)} %bitcast.177, f32[1536,360]{0,1:T(8,128)} %fusion.35, bf16[1,2304,360]{1,2,0:T(8,128)(2,1)} %param.38), kind=kOutput, calls=%fused_computation.12 | convolution fusion | flops 5102936064 | bytes 19685376 | tf_op jit(solution)/shard_map/dot_general | solution.py:214
  335.9 3.6 gather_fusion.6
  339.9 73.2 %reduce-scatter.6.cloned.1.call-done = bf16[96,2304]{1,0:T(8,128)(2,1)} async-done(((bf16[1536,2304]{1,0:T(8,128)(2,1)}), bf16[96,2304]{1,0:T(8,128)(2,1)}) %reduce-scatter.6.cloned.1.call-update) | async-done | bytes 442384 | tf_op jit(solution)/shard_map/reduce_scatter | solution.py:219
  413.2 3.2 convolution_convert_fusion.3
  417.2 30.7 %reduce-scatter.8.cloned.1.call-done = bf16[32,2304]{1,0:T(8,128)(2,1)} async-done(((bf16[256,2304]{1,0:T(8,128)(2,1)}), bf16[32,2304]{1,0:T(8,128)(2,1)}) %reduce-scatter.8.cloned.1.call-update) | async-done | bytes 147472 | tf_op jit(solution)/shard_map/reduce_scatter | solution.py:224
  (176 shorter events, 74.7 us)
Async XLA Ops:
  6.5 314.0 %copy-start = (bf16[1,360,2304]{2,1,0:T(8,128)(2,1)S(1)}, bf16[1,360,2304]{2,1,0:T(8,128)(2,1)}, u32[]{:S(2)}) copy-start(bf16[1,360,2304]{2,1,0:T(8,128)(2,1)} %param.39) | copy-start | bytes 4976644
  6.5 116.0 %all-gather.3.cloned.1.call-start = ((), (), s32[]{:S(2)}) async-start(), calls=%async_computation.6 | async-start | bytes 4456448 | tf_op jit(solution)/shard_map/all_gather | solution.py:99
  12.7 10.4 %copy-start.27 = (u32[128]{0:T(128)S(1)}, u32[128]{0:T(128)}, u32[]{:S(2)}) copy-start(u32[128]{0:T(128)} %constant.214) | copy-start | bytes 1540
  12.7 11.7 %copy-start.24 = (s32[8]{0:T(128)S(1)}, s32[8]{0:T(128)}, u32[]{:S(2)}) copy-start(s32[8]{0:T(128)} %param.31) | copy-start | bytes 100
  12.7 29.3 %copy-start.2 = (s32[8]{0:T(128)S(1)}, s32[8]{0:T(128)}, u32[]{:S(2)}) copy-start(s32[8]{0:T(128)} %param.33) | copy-start | bytes 100
  12.7 29.3 %copy-start.23 = (s32[2]{0:T(128)S(1)}, s32[2]{0:T(128)}, u32[]{:S(2)}) copy-start(s32[2]{0:T(128)} %param.30) | copy-start | bytes 28
  14.0 33.2 %copy-start.6 = (bf16[256,2304]{1,0:T(8,128)(2,1)S(1)}, bf16[256,2304]{1,0:T(8,128)(2,1)}, u32[]{:S(2)}) copy-start(bf16[256,2304]{1,0:T(8,128)(2,1)} %param.20) | copy-start | bytes 3538948
  14.9 47.3 %all-to-all-start = ((bf16[16,2,32,256]{3,2,1,0:T(8,128)(2,1)}), bf16[16,2,32,256]{3,2,1,0:T(8,128)(2,1)}, u32[]{:S(2)}, u32[]{:S(2)}) async-start(bf16[16,2,32,256]{3,2,1,0:T(8,128)(2,1)} %pad_maximum_fusion.1), calls=%async_computation | async-start | bytes 1048576 | tf_op jit(solution)/shard_map/all_to_all | solution.py:154
  44.9 4.7 %copy-start.7 = (bf16[2,2,1024,256]{3,2,1,0:T(8,128)(2,1)S(1)}, bf16[2,2,1024,256]{3,2,1,0:T(8,128)(2,1)}, u32[]{:S(2)}) copy-start(bf16[2,2,1024,256]{3,2,1,0:T(8,128)(2,1)} %param.28) | copy-start | bytes 6291460
  49.7 3.9 copy-start.9
  53.8 4.2 copy-start.10
  53.8 6.4 %copy-start.18 = (bf16[8,32,4,64]{3,2,1,0:T(4,128)(2,1)S(1)}, bf16[8,32,4,64]{3,2,1,0:T(4,128)(2,1)}, u32[]{:S(2)}) copy-start(bf16[8,32,4,64]{3,2,1,0:T(4,128)(2,1)} %reshape.409) | copy-start | bytes 393220
  87.6 6.6 %copy-start.26 = (f32[2304]{0:T(1024)S(1)}, f32[2304]{0:T(1024)}, u32[]{:S(2)}) copy-start(f32[2304]{0:T(1024)} %param.21) | copy-start | bytes 27652
  87.6 25.6 %all-to-all-start.1 = ((f32[16,2,32,260]{3,2,1,0:T(8,128)}), f32[16,2,32,260]{3,2,1,0:T(8,128)S(1)}, u32[]{:S(2)}, u32[]{:S(2)}) async-start(f32[16,2,32,260]{3,2,1,0:T(8,128)} %pad_maximum_fusion), calls=%async_computation.1 | async-start | bytes 3145728 | tf_op jit(solution)/shard_map/all_to_all | solution.py:172
  92.7 104.0 %reduce-scatter.4.cloned.1.call-start = ((), (), s32[]{:S(2)}) async-start(), calls=%async_computation.7 | async-start | bytes 2654208 | tf_op jit(solution)/shard_map/reduce_scatter | solution.py:188
  131.1 4.2 copy-start.17
  153.6 8.2 %copy-start.12 = (f32[1,256,4,64]{1,3,2,0:T(8,128)S(1)}, f32[1,256,4,64]{1,3,2,0:T(8,128)}, u32[]{:S(2)}) copy-start(f32[1,256,4,64]{1,3,2,0:T(8,128)} %copy.288) | copy-start | bytes 786436
  163.0 34.8 %copy-start.22 = (f32[2304]{0:T(1024)S(1)}, f32[2304]{0:T(1024)}, u32[]{:S(2)}) copy-start(f32[2304]{0:T(1024)} %param.34) | copy-start | bytes 27652
  164.9 35.0 %copy-start.21 = (s32[256,2]{0,1:T(2,128)S(1)}, s32[256,2]{0,1:T(2,128)}, u32[]{:S(2)}) copy-start(s32[256,2]{0,1:T(2,128)} %param.36) | copy-start | bytes 6148
  164.9 57.4 %all-gather.5.cloned.1.call-start = ((), (), s32[]{:S(2)}) async-start(), calls=%async_computation.8 | async-start | bytes 1327104 | tf_op jit(solution)/shard_map/all_gather | solution.py:191
  199.6 213.6 %reduce-scatter.6.cloned.1.call-start = ((), (), s32[]{:S(2)}) async-start(), calls=%async_computation.9 | async-start | bytes 7520256 | tf_op jit(solution)/shard_map/reduce_scatter | solution.py:219
  224.6 91.8 %copy-start.25 = (bf16[1,2304,360]{1,2,0:T(8,128)(2,1)S(1)}, bf16[1,2304,360]{1,2,0:T(8,128)(2,1)}, u32[]{:S(2)}) copy-start(bf16[1,2304,360]{1,2,0:T(8,128)(2,1)} %param.37) | copy-start | bytes 4976644
  333.7 114.2 %reduce-scatter.8.cloned.1.call-start = ((), (), s32[]{:S(2)}) async-start(), calls=%async_computation.10 | async-start | bytes 1327104 | tf_op jit(solution)/shard_map/reduce_scatter | solution.py:224
  339.5 108.4 %copy-start.5 = (f32[32,2304]{1,0:T(8,128)S(1)}, f32[32,2304]{1,0:T(8,128)}, u32[]{:S(2)}) copy-start(f32[32,2304]{1,0:T(8,128)} %reduce-scatter.4.cloned.1.call-done) | copy-start | bytes 884740
  (11 other events, 22.8 us)
Sparse Core Ops, SparseCore 0:
  9.6 57.6 all-gather.2
  165.0 31.5 reduce-scatter.3
  199.7 22.5 all-gather.4
  333.8 79.3 reduce-scatter.5
  416.5 31.2 reduce-scatter.7
